TPU v7x, 32 devices: a whole 2x2x4 slice. The times are simulated.
32 devices in a mesh: wl: 4 (over x, core), gx: 2 (over y), gy: 4 (over z).
Axes of the slice: x: 2, y: 2, z: 4, core: 2. Of those that a mesh axis runs over, the one named last changes fastest.
Arguments:
- forward_efield: float32 [4, 3, 64, 32, 128], P('wl', None, 'gx', 'gy'), may hold values from -6 to 6
- forward_hfield: float32 [4, 3, 64, 32, 128], P('wl', None, 'gx', 'gy'), may hold values from -6 to 6
- adjoint_efield: float32 [4, 3, 64, 32, 128], P('wl', None, 'gx', 'gy'), may hold values from -6 to 6
- adjoint_hfield: float32 [4, 3, 64, 32, 128], P('wl', None, 'gx', 'gy'), may hold values from -6 to 6
- background: float32 [64, 32, 128], P('gx', 'gy'), may hold values from 1 to 4
- design: float32 [8, 64, 32], P('wl', 'gx', 'gy'), may hold values from 1.5 to 6
- source_profile: float32 [4, 64, 32], P('wl', 'gx', 'gy'), may hold values from -24 to 24
- source_layer: int32 [4], P('wl'), may hold values from 4 to 59
- monitor_layer: int32 [4], P('wl'), may hold values from 76 to 123
Outputs:
- final_forward: float32 [4, 3, 64, 32, 128], P('wl', None, 'gx', 'gy')
- final_adjoint: float32 [4, 3, 64, 32, 128], P('wl', None, 'gx', 'gy')
- gradient: float32 [8, 64, 32], P('wl', 'gx', 'gy')
Inputs may be any that keep to these rules, and one draw needn't show every extreme that they name: `source_layer`: a z layer below the design slab. `monitor_layer`: a z layer above the design slab.
All inputs are finite; a program needn't handle non-finite values.
Results may differ from a plain program's by a relative error of at most 0.0001.
Values sent between devices are 32-bit elements; how exact they have to be, the bound alone decides.
No kernel may reach another device: no remote copies, remote signals or barrier semaphores. Data moves between devices by JAX's collectives and lax.ppermute only.
A program may use at most 64 MiB of HBM per device.

v0:
```python
import math
import jax
import jax.numpy as jnp
from jax import lax
from jax.sharding import PartitionSpec as P

Z0 = 64
STEPS = 3
time_step = 0.5


def shifted_2(block, axis, distance):
    devices = range(lax.axis_size(axis))
    route = [(i - distance, i) for i in devices if i - distance in devices]
    return lax.ppermute(block, axis, route)


def neighbours(stacked, upward):
    offset = -1 if upward else 1
    plane_x = stacked[:, :1] if upward else stacked[:, -1:]
    plane_y = stacked[:, :, :1] if upward else stacked[:, :, -1:]
    got_x = shifted_2(plane_x, "gx", offset)
    got_y = shifted_2(plane_y, "gy", offset)
    return (got_x, got_y)


def along(stacked, axis, edge, upward):
    count = stacked.shape[axis]
    if upward:
        shifted = jnp.concatenate([lax.slice_in_dim(stacked, 1, count, axis=axis), edge], axis=axis)
        return shifted - stacked
    shifted = jnp.concatenate([edge, lax.slice_in_dim(stacked, 0, count - 1, axis=axis)], axis=axis)
    return stacked - shifted


def curl(stacked, upward):
    comps, width, height, depth = stacked.shape
    edge_x, edge_y = neighbours(stacked, upward)
    edge_z = jnp.zeros((comps, width, height, 1), jnp.float32)
    along_x = along(stacked, 1, edge_x, upward)
    along_y = along(stacked, 2, edge_y, upward)
    along_z = along(stacked, 3, edge_z, upward)
    return jnp.stack([along_y[2] - along_z[1], along_z[0] - along_x[2], along_x[1] - along_y[0]])


def run_window(efield, hfield, adj_e, adj_h, coef, source_term, omega, monitor_mask, slab_depth):
    slabs = []
    monitors = []
    monitor_pick = monitor_mask[None, None, None, :]
    for turn in range(STEPS):
        hfield = hfield - time_step * curl(efield, True)
        efield = efield + coef * curl(hfield, False)
        signal = jnp.sin(omega * ((turn + 1) * time_step))
        efield = efield.at[0].add(time_step * signal * source_term)
        slabs.append(efield[:, :, :, Z0 : Z0 + slab_depth])
        monitors.append(jnp.sum(efield * monitor_pick, axis=3, keepdims=True))
    total = jnp.zeros((efield.shape[1], efield.shape[2], slab_depth), jnp.float32)
    for turn in range(STEPS):
        adj_h = adj_h - time_step * curl(adj_e, True)
        adj_e = adj_e + coef * curl(adj_h, False)
        adj_e = adj_e + 2.0 * time_step * monitors[STEPS - 1 - turn] * monitor_mask
        total = total + jnp.sum(
            slabs[STEPS - 1 - turn] * adj_e[:, :, :, Z0 : Z0 + slab_depth], axis=0
        )
    return (efield, adj_e, total)


def per_device(
    forward_efield,
    forward_hfield,
    adjoint_efield,
    adjoint_hfield,
    background,
    design,
    source_profile,
    source_layer,
    monitor_layer,
):
    groups = lax.axis_size("wl")
    owned = design.shape[0]
    slab_depth = owned * groups
    depth = background.shape[2]
    tiles = lax.all_gather(design, "wl", axis=0, tiled=True)
    permit = jnp.concatenate(
        [
            background[:, :, :Z0],
            jnp.transpose(tiles, (1, 2, 0)),
            background[:, :, Z0 + slab_depth :],
        ],
        axis=2,
    )
    layers = lax.iota(jnp.int32, depth)
    wave_index = lax.axis_index("wl").astype(jnp.float32)
    omega = jnp.float32(2.0 * math.pi) / (16.0 + 32.0 * wave_index / groups)
    source_mask = (layers == source_layer[0]).astype(jnp.float32)
    monitor_mask = (layers == monitor_layer[0]).astype(jnp.float32)
    source_term = source_profile[0][:, :, None] * source_mask
    coef = time_step / permit
    efield, adj_e, total = run_window(
        forward_efield[0],
        forward_hfield[0],
        adjoint_efield[0],
        adjoint_hfield[0],
        coef,
        source_term,
        omega,
        monitor_mask,
        slab_depth,
    )
    local_grad = jnp.transpose(omega * omega * total, (2, 0, 1))
    summed = lax.psum(local_grad, "wl")
    gradient = lax.dynamic_slice_in_dim(summed, lax.axis_index("wl") * owned, owned, 0)
    return (efield[None], adj_e[None], gradient)


def solution(mesh):
    return jax.shard_map(
        per_device,
        mesh=mesh,
        in_specs=(
            P("wl", None, "gx", "gy", None),
            P("wl", None, "gx", "gy", None),
            P("wl", None, "gx", "gy", None),
            P("wl", None, "gx", "gy", None),
            P("gx", "gy", None),
            P("wl", "gx", "gy"),
            P("wl", "gx", "gy"),
            P("wl"),
            P("wl"),
        ),
        out_specs=(
            P("wl", None, "gx", "gy", None),
            P("wl", None, "gx", "gy", None),
            P("wl", "gx", "gy"),
        ),
        check_vma=False,
    )
```

profile of v0, /device:TPU:0, one launch (start us, length us, event | category | flops | bytes accessed | tf_op | source)
XLA Modules:
  0.0 120.3 jit_solution(9037135590626028653)
XLA Ops:
  0.6 1.0 slice.645
  1.7 1.3 %collective-permute-start = (f32[3,32,1,128]{3,2,1,0:T(1,128)S(1)}, f32[3,32,1,128]{3,2,1,0:T(1,128)S(1)}, u32[]{:S(2)}, u32[]{:S(2)}) collective-permute-start(f32[3,32,1,128]{3,2,1,0:T(1,128)S(1)} %slice.645), channel_id=1, source_target_pairs={{1,0},{2,1},{3,2},{5,4},{6,5},{7,6},{9,8},{10,9},{11,10},{13,12},{... | collective-permute-start | bytes 147464 | tf_op jit(solution)/shard_map/ppermute | solution.py:15
  3.0 0.7 slice.651
  3.7 1.3 %collective-permute-start.1 = (f32[3,1,8,128]{3,2,1,0:T(8,128)S(1)}, f32[3,1,8,128]{3,2,1,0:T(8,128)S(1)}, u32[]{:S(2)}, u32[]{:S(2)}) collective-permute-start(f32[3,1,8,128]{3,2,1,0:T(8,128)S(1)} %slice.651), channel_id=1, source_target_pairs={{4,0},{5,1},{6,2},{7,3},{12,8},{13,9},{14,10},{15,11},{20,16},{21,... | collective-permute-start | bytes 36872 | tf_op jit(solution)/shard_map/ppermute | solution.py:15
  5.0 1.0 slice.714
  6.0 1.4 %collective-permute-start.12 = (f32[3,32,1,128]{3,2,1,0:T(1,128)S(1)}, f32[3,32,1,128]{3,2,1,0:T(1,128)S(1)}, u32[]{:S(2)}, u32[]{:S(2)}) collective-permute-start(f32[3,32,1,128]{3,2,1,0:T(1,128)S(1)} %slice.714), channel_id=1, source_target_pairs={{1,0},{2,1},{3,2},{5,4},{6,5},{7,6},{9,8},{10,9},{11,10},{13,12},{... | collective-permute-start | bytes 147464 | tf_op jit(solution)/shard_map/ppermute | solution.py:15
  7.4 0.7 slice.720
  8.2 1.3 %collective-permute-start.13 = (f32[3,1,8,128]{3,2,1,0:T(8,128)S(1)}, f32[3,1,8,128]{3,2,1,0:T(8,128)S(1)}, u32[]{:S(2)}, u32[]{:S(2)}) collective-permute-start(f32[3,1,8,128]{3,2,1,0:T(8,128)S(1)} %slice.720), channel_id=1, source_target_pairs={{4,0},{5,1},{6,2},{7,3},{12,8},{13,9},{14,10},{15,11},{20,16},{21,... | collective-permute-start | bytes 36872 | tf_op jit(solution)/shard_map/ppermute | solution.py:15
  9.5 6.2 %all_gather.3 = f32[8,32,8]{1,2,0:T(8,128)S(1)} all-gather(f32[2,32,8]{1,2,0:T(8,128)S(1)} %copy-done.26), channel_id=1, replica_groups=mesh['wl'=4,'gx'=2,'gy'=4] {'wl'}, dimensions={0}, use_global_device_ids=true | all-gather | bytes 10240 | tf_op jit(solution)/shard_map/all_gather | solution.py:83
  17.4 0.2 slice.647
  17.6 1.0 copy-done
  19.1 0.6 copy-done.27
  20.1 0.9 copy-done.1
  21.1 5.2 %collective-permute-start.2 = (f32[3,32,1,128]{3,2,1,0:T(1,128)S(1)}, f32[3,32,1,128]{3,2,1,0:T(1,128)S(1)}, u32[]{:S(2)}, u32[]{:S(2)}) collective-permute-start(f32[3,32,1,128]{3,2,1,0:T(1,128)S(1)} %slice.655), channel_id=1, source_target_pairs={{0,1},{1,2},{2,3},{4,5},{5,6},{6,7},{8,9},{9,10},{10,11},{12,13},{... | collective-permute-start | bytes 147464 | tf_op jit(solution)/shard_map/ppermute | solution.py:15
  26.3 4.5 %collective-permute-start.3 = (f32[3,1,8,128]{3,2,1,0:T(8,128)S(1)}, f32[3,1,8,128]{3,2,1,0:T(8,128)S(1)}, u32[]{:S(2)}, u32[]{:S(2)}) collective-permute-start(f32[3,1,8,128]{3,2,1,0:T(8,128)S(1)} %slice.661), channel_id=1, source_target_pairs={{0,4},{1,5},{2,6},{3,7},{8,12},{9,13},{10,14},{11,15},{16,20},{17,... | collective-permute-start | bytes 36872 | tf_op jit(solution)/shard_map/ppermute | solution.py:15
  31.1 1.2 collective-permute-done.3
  32.3 0.2 pad_subtract_fusion.10
  32.7 1.3 %collective-permute-start.4 = (f32[3,32,1,128]{3,2,1,0:T(1,128)S(1)}, f32[3,32,1,128]{3,2,1,0:T(1,128)S(1)}, u32[]{:S(2)}, u32[]{:S(2)}) collective-permute-start(f32[3,32,1,128]{3,2,1,0:T(1,128)S(1)} %slice.668), channel_id=1, source_target_pairs={{1,0},{2,1},{3,2},{5,4},{6,5},{7,6},{9,8},{10,9},{11,10},{13,12},{... | collective-permute-start | bytes 147464 | tf_op jit(solution)/shard_map/ppermute | solution.py:15
  34.0 1.3 %collective-permute-start.5 = (f32[3,1,8,128]{3,2,1,0:T(8,128)S(1)}, f32[3,1,8,128]{3,2,1,0:T(8,128)S(1)}, u32[]{:S(2)}, u32[]{:S(2)}) collective-permute-start(f32[3,1,8,128]{3,2,1,0:T(8,128)S(1)} %slice.674), channel_id=1, source_target_pairs={{4,0},{5,1},{6,2},{7,3},{12,8},{13,9},{14,10},{15,11},{20,16},{21,... | collective-permute-start | bytes 36872 | tf_op jit(solution)/shard_map/ppermute | solution.py:15
  35.4 0.2 slice.670
  35.6 4.0 %collective-permute-done.5 = f32[3,1,8,128]{3,2,1,0:T(8,128)S(1)} collective-permute-done((f32[3,1,8,128]{3,2,1,0:T(8,128)S(1)}, f32[3,1,8,128]{3,2,1,0:T(8,128)S(1)}, u32[]{:S(2)}, u32[]{:S(2)}) %collective-permute-start.5) | collective-permute-done | bytes 12320 | tf_op jit(solution)/shard_map/ppermute | solution.py:15
  40.0 4.6 %collective-permute-start.6 = (f32[3,32,1,128]{3,2,1,0:T(1,128)S(1)}, f32[3,32,1,128]{3,2,1,0:T(1,128)S(1)}, u32[]{:S(2)}, u32[]{:S(2)}) collective-permute-start(f32[3,32,1,128]{3,2,1,0:T(1,128)S(1)} %slice.678), channel_id=1, source_target_pairs={{0,1},{1,2},{2,3},{4,5},{5,6},{6,7},{8,9},{9,10},{10,11},{12,13},{... | collective-permute-start | bytes 147464 | tf_op jit(solution)/shard_map/ppermute | solution.py:15
  44.5 2.7 %collective-permute-start.7 = (f32[3,1,8,128]{3,2,1,0:T(8,128)S(1)}, f32[3,1,8,128]{3,2,1,0:T(8,128)S(1)}, u32[]{:S(2)}, u32[]{:S(2)}) collective-permute-start(f32[3,1,8,128]{3,2,1,0:T(8,128)S(1)} %slice.684), channel_id=1, source_target_pairs={{0,4},{1,5},{2,6},{3,7},{8,12},{9,13},{10,14},{11,15},{16,20},{17,... | collective-permute-start | bytes 36872 | tf_op jit(solution)/shard_map/ppermute | solution.py:15
  47.4 3.9 %collective-permute-start.14 = (f32[3,32,1,128]{3,2,1,0:T(1,128)S(1)}, f32[3,32,1,128]{3,2,1,0:T(1,128)S(1)}, u32[]{:S(2)}, u32[]{:S(2)}) collective-permute-start(f32[3,32,1,128]{3,2,1,0:T(1,128)S(1)} %slice.724), channel_id=1, source_target_pairs={{0,1},{1,2},{2,3},{4,5},{5,6},{6,7},{8,9},{9,10},{10,11},{12,13},{... | collective-permute-start | bytes 147464 | tf_op jit(solution)/shard_map/ppermute | solution.py:15
  51.3 1.3 %collective-permute-start.15 = (f32[3,1,8,128]{3,2,1,0:T(8,128)S(1)}, f32[3,1,8,128]{3,2,1,0:T(8,128)S(1)}, u32[]{:S(2)}, u32[]{:S(2)}) collective-permute-start(f32[3,1,8,128]{3,2,1,0:T(8,128)S(1)} %slice.730), channel_id=1, source_target_pairs={{0,4},{1,5},{2,6},{3,7},{8,12},{9,13},{10,14},{11,15},{16,20},{17,... | collective-permute-start | bytes 36872 | tf_op jit(solution)/shard_map/ppermute | solution.py:15
  52.6 0.2 pad_subtract_fusion.8
  53.1 1.3 %collective-permute-start.8 = (f32[3,32,1,128]{3,2,1,0:T(1,128)S(1)}, f32[3,32,1,128]{3,2,1,0:T(1,128)S(1)}, u32[]{:S(2)}, u32[]{:S(2)}) collective-permute-start(f32[3,32,1,128]{3,2,1,0:T(1,128)S(1)} %slice.691), channel_id=1, source_target_pairs={{1,0},{2,1},{3,2},{5,4},{6,5},{7,6},{9,8},{10,9},{11,10},{13,12},{... | collective-permute-start | bytes 147464 | tf_op jit(solution)/shard_map/ppermute | solution.py:15
  54.4 1.3 %collective-permute-start.9 = (f32[3,1,8,128]{3,2,1,0:T(8,128)S(1)}, f32[3,1,8,128]{3,2,1,0:T(8,128)S(1)}, u32[]{:S(2)}, u32[]{:S(2)}) collective-permute-start(f32[3,1,8,128]{3,2,1,0:T(8,128)S(1)} %slice.697), channel_id=1, source_target_pairs={{4,0},{5,1},{6,2},{7,3},{12,8},{13,9},{14,10},{15,11},{20,16},{21,... | collective-permute-start | bytes 36872 | tf_op jit(solution)/shard_map/ppermute | solution.py:15
  55.8 0.2 pad_subtract_fusion.4
  56.2 3.8 %collective-permute-done.9 = f32[3,1,8,128]{3,2,1,0:T(8,128)S(1)} collective-permute-done((f32[3,1,8,128]{3,2,1,0:T(8,128)S(1)}, f32[3,1,8,128]{3,2,1,0:T(8,128)S(1)}, u32[]{:S(2)}, u32[]{:S(2)}) %collective-permute-start.9) | collective-permute-done | bytes 12320 | tf_op jit(solution)/shard_map/ppermute | solution.py:15
  60.4 4.5 %collective-permute-start.10 = (f32[3,32,1,128]{3,2,1,0:T(1,128)S(1)}, f32[3,32,1,128]{3,2,1,0:T(1,128)S(1)}, u32[]{:S(2)}, u32[]{:S(2)}) collective-permute-start(f32[3,32,1,128]{3,2,1,0:T(1,128)S(1)} %slice.701), channel_id=1, source_target_pairs={{0,1},{1,2},{2,3},{4,5},{5,6},{6,7},{8,9},{9,10},{10,11},{12,13},{... | collective-permute-start | bytes 147464 | tf_op jit(solution)/shard_map/ppermute | solution.py:15
  64.9 1.6 %collective-permute-start.11 = (f32[3,1,8,128]{3,2,1,0:T(8,128)S(1)}, f32[3,1,8,128]{3,2,1,0:T(8,128)S(1)}, u32[]{:S(2)}, u32[]{:S(2)}) collective-permute-start(f32[3,1,8,128]{3,2,1,0:T(8,128)S(1)} %slice.707), channel_id=1, source_target_pairs={{0,4},{1,5},{2,6},{3,7},{8,12},{9,13},{10,14},{11,15},{16,20},{17,... | collective-permute-start | bytes 36872 | tf_op jit(solution)/shard_map/ppermute | solution.py:15
  66.7 1.3 %collective-permute-done.11 = f32[3,1,8,128]{3,2,1,0:T(8,128)S(1)} collective-permute-done((f32[3,1,8,128]{3,2,1,0:T(8,128)S(1)}, f32[3,1,8,128]{3,2,1,0:T(8,128)S(1)}, u32[]{:S(2)}, u32[]{:S(2)}) %collective-permute-start.11) | collective-permute-done | bytes 12320 | tf_op jit(solution)/shard_map/ppermute | solution.py:15
  68.0 0.3 pad_subtract_fusion.6
  68.5 0.8 multiply_reduce_fusion
  69.3 0.2 fusion.21
  69.5 1.3 %collective-permute-start.16 = (f32[3,32,1,128]{3,2,1,0:T(1,128)S(1)}, f32[3,32,1,128]{3,2,1,0:T(1,128)S(1)}, u32[]{:S(2)}, u32[]{:S(2)}) collective-permute-start(f32[3,32,1,128]{3,2,1,0:T(1,128)S(1)} %slice.736), channel_id=1, source_target_pairs={{1,0},{2,1},{3,2},{5,4},{6,5},{7,6},{9,8},{10,9},{11,10},{13,12},{... | collective-permute-start | bytes 147464 | tf_op jit(solution)/shard_map/ppermute | solution.py:15
  70.8 1.3 %collective-permute-start.17 = (f32[3,1,8,128]{3,2,1,0:T(8,128)S(1)}, f32[3,1,8,128]{3,2,1,0:T(8,128)S(1)}, u32[]{:S(2)}, u32[]{:S(2)}) collective-permute-start(f32[3,1,8,128]{3,2,1,0:T(8,128)S(1)} %slice.742), channel_id=1, source_target_pairs={{4,0},{5,1},{6,2},{7,3},{12,8},{13,9},{14,10},{15,11},{20,16},{21,... | collective-permute-start | bytes 36872 | tf_op jit(solution)/shard_map/ppermute | solution.py:15
  72.4 4.0 %collective-permute-done.17 = f32[3,1,8,128]{3,2,1,0:T(8,128)S(1)} collective-permute-done((f32[3,1,8,128]{3,2,1,0:T(8,128)S(1)}, f32[3,1,8,128]{3,2,1,0:T(8,128)S(1)}, u32[]{:S(2)}, u32[]{:S(2)}) %collective-permute-start.17) | collective-permute-done | bytes 12320 | tf_op jit(solution)/shard_map/ppermute | solution.py:15
  76.4 0.2 pad_subtract_fusion.3
  76.9 4.5 %collective-permute-start.18 = (f32[3,32,1,128]{3,2,1,0:T(1,128)S(1)}, f32[3,32,1,128]{3,2,1,0:T(1,128)S(1)}, u32[]{:S(2)}, u32[]{:S(2)}) collective-permute-start(f32[3,32,1,128]{3,2,1,0:T(1,128)S(1)} %slice.746), channel_id=1, source_target_pairs={{0,1},{1,2},{2,3},{4,5},{5,6},{6,7},{8,9},{9,10},{10,11},{12,13},{... | collective-permute-start | bytes 147464 | tf_op jit(solution)/shard_map/ppermute | solution.py:15
  81.4 1.6 %collective-permute-start.19 = (f32[3,1,8,128]{3,2,1,0:T(8,128)S(1)}, f32[3,1,8,128]{3,2,1,0:T(8,128)S(1)}, u32[]{:S(2)}, u32[]{:S(2)}) collective-permute-start(f32[3,1,8,128]{3,2,1,0:T(8,128)S(1)} %slice.752), channel_id=1, source_target_pairs={{0,4},{1,5},{2,6},{3,7},{8,12},{9,13},{10,14},{11,15},{16,20},{17,... | collective-permute-start | bytes 36872 | tf_op jit(solution)/shard_map/ppermute | solution.py:15
  83.1 1.4 %collective-permute-done.19 = f32[3,1,8,128]{3,2,1,0:T(8,128)S(1)} collective-permute-done((f32[3,1,8,128]{3,2,1,0:T(8,128)S(1)}, f32[3,1,8,128]{3,2,1,0:T(8,128)S(1)}, u32[]{:S(2)}, u32[]{:S(2)}) %collective-permute-start.19) | collective-permute-done | bytes 12320 | tf_op jit(solution)/shard_map/ppermute | solution.py:15
  84.5 0.2 pad_subtract_fusion.2
  84.8 0.3 fusion.24
  85.1 0.3 copy-done.8
  85.5 0.6 slice.758
  86.1 1.3 %collective-permute-start.20 = (f32[3,32,1,128]{3,2,1,0:T(1,128)}, f32[3,32,1,128]{3,2,1,0:T(1,128)}, u32[]{:S(2)}, u32[]{:S(2)}) collective-permute-start(f32[3,32,1,128]{3,2,1,0:T(1,128)} %slice.758), channel_id=1, source_target_pairs={{1,0},{2,1},{3,2},{5,4},{6,5},{7,6},{9,8},{10,9},{11,10},{13,12},{... | collective-permute-start | bytes 147464 | tf_op jit(solution)/shard_map/ppermute | solution.py:15
  87.4 1.3 %collective-permute-start.21 = (f32[3,1,8,128]{3,2,1,0:T(8,128)S(1)}, f32[3,1,8,128]{3,2,1,0:T(8,128)}, u32[]{:S(2)}, u32[]{:S(2)}) collective-permute-start(f32[3,1,8,128]{3,2,1,0:T(8,128)S(1)} %slice.764), channel_id=1, source_target_pairs={{4,0},{5,1},{6,2},{7,3},{12,8},{13,9},{14,10},{15,11},{20,16},{21,... | collective-permute-start | bytes 36872 | tf_op jit(solution)/shard_map/ppermute | solution.py:15
  88.7 0.8 slice.784
  89.5 0.6 slice.786
  90.4 2.8 %collective-permute-done.21 = f32[3,1,8,128]{3,2,1,0:T(8,128)} collective-permute-done((f32[3,1,8,128]{3,2,1,0:T(8,128)S(1)}, f32[3,1,8,128]{3,2,1,0:T(8,128)}, u32[]{:S(2)}, u32[]{:S(2)}) %collective-permute-start.21) | collective-permute-done | bytes 12320 | tf_op jit(solution)/shard_map/ppermute | solution.py:15
  93.2 1.2 pad_subtract_fusion.1
  94.4 0.8 copy-done.7
  95.4 4.5 %collective-permute-start.22 = (f32[3,32,1,128]{3,2,1,0:T(1,128)S(1)}, f32[3,32,1,128]{3,2,1,0:T(1,128)S(1)}, u32[]{:S(2)}, u32[]{:S(2)}) collective-permute-start(f32[3,32,1,128]{3,2,1,0:T(1,128)S(1)} %slice.768), channel_id=1, source_target_pairs={{0,1},{1,2},{2,3},{4,5},{5,6},{6,7},{8,9},{9,10},{10,11},{12,13},{... | collective-permute-start | bytes 147464 | tf_op jit(solution)/shard_map/ppermute | solution.py:15
  100.0 3.3 %collective-permute-start.23 = (f32[3,1,8,128]{3,2,1,0:T(8,128)S(1)}, f32[3,1,8,128]{3,2,1,0:T(8,128)S(1)}, u32[]{:S(2)}, u32[]{:S(2)}) collective-permute-start(f32[3,1,8,128]{3,2,1,0:T(8,128)S(1)} %slice.774), channel_id=1, source_target_pairs={{0,4},{1,5},{2,6},{3,7},{8,12},{9,13},{10,14},{11,15},{16,20},{17,... | collective-permute-start | bytes 36872 | tf_op jit(solution)/shard_map/ppermute | solution.py:15
  103.3 0.3 fusion.6
  103.6 1.1 collective-permute-done.23
  104.7 0.3 pad_subtract_fusion
  105.0 0.8 copy-done.23
  105.8 0.6 fusion.5
  106.5 11.6 %psum.7 = f32[8,32,8]{0,2,1:T(8,128)S(1)} all-reduce(f32[8,32,8]{0,2,1:T(8,128)S(1)} %multiply_bitcast_fusion), channel_id=1, replica_groups=mesh['wl'=4,'gx'=2,'gy'=4] {'wl'}, use_global_device_ids=true, to_apply=%region_6.0 | all-reduce | flops 2048 | bytes 16384 | tf_op jit(solution)/shard_map/psum | solution.py:111
  118.2 0.7 copy.16
  119.1 1.1 fusion.19
  (145 shorter events, 4.6 us)
Async XLA Ops:
  1.7 18.2 %collective-permute-start = (f32[3,32,1,128]{3,2,1,0:T(1,128)S(1)}, f32[3,32,1,128]{3,2,1,0:T(1,128)S(1)}, u32[]{:S(2)}, u32[]{:S(2)}) collective-permute-start(f32[3,32,1,128]{3,2,1,0:T(1,128)S(1)} %slice.645), channel_id=1, source_target_pairs={{1,0},{2,1},{3,2},{5,4},{6,5},{7,6},{9,8},{10,9},{11,10},{13,12},{... | collective-permute-start | bytes 147464 | tf_op jit(solution)/shard_map/ppermute | solution.py:15
  3.7 16.2 %collective-permute-start.1 = (f32[3,1,8,128]{3,2,1,0:T(8,128)S(1)}, f32[3,1,8,128]{3,2,1,0:T(8,128)S(1)}, u32[]{:S(2)}, u32[]{:S(2)}) collective-permute-start(f32[3,1,8,128]{3,2,1,0:T(8,128)S(1)} %slice.651), channel_id=1, source_target_pairs={{4,0},{5,1},{6,2},{7,3},{12,8},{13,9},{14,10},{15,11},{20,16},{21,... | collective-permute-start | bytes 36872 | tf_op jit(solution)/shard_map/ppermute | solution.py:15
  5.0 4.5 %copy-start.26 = (f32[2,32,8]{1,2,0:T(8,128)S(1)}, f32[2,32,8]{1,2,0:T(8,128)}, u32[]{:S(2)}) copy-start(f32[2,32,8]{1,2,0:T(8,128)} %param.20) | copy-start | bytes 6148
  6.0 9.8 %copy-start.24 = (f32[32,8,128]{2,1,0:T(8,128)S(1)}, f32[32,8,128]{2,1,0:T(8,128)}, u32[]{:S(2)}) copy-start(f32[32,8,128]{2,1,0:T(8,128)} %param.19) | copy-start | bytes 393220
  6.0 24.9 %collective-permute-start.12 = (f32[3,32,1,128]{3,2,1,0:T(1,128)S(1)}, f32[3,32,1,128]{3,2,1,0:T(1,128)S(1)}, u32[]{:S(2)}, u32[]{:S(2)}) collective-permute-start(f32[3,32,1,128]{3,2,1,0:T(1,128)S(1)} %slice.714), channel_id=1, source_target_pairs={{1,0},{2,1},{3,2},{5,4},{6,5},{7,6},{9,8},{10,9},{11,10},{13,12},{... | collective-permute-start | bytes 147464 | tf_op jit(solution)/shard_map/ppermute | solution.py:15
  8.2 22.7 %collective-permute-start.13 = (f32[3,1,8,128]{3,2,1,0:T(8,128)S(1)}, f32[3,1,8,128]{3,2,1,0:T(8,128)S(1)}, u32[]{:S(2)}, u32[]{:S(2)}) collective-permute-start(f32[3,1,8,128]{3,2,1,0:T(8,128)S(1)} %slice.720), channel_id=1, source_target_pairs={{4,0},{5,1},{6,2},{7,3},{12,8},{13,9},{14,10},{15,11},{20,16},{21,... | collective-permute-start | bytes 36872 | tf_op jit(solution)/shard_map/ppermute | solution.py:15
  15.8 1.6 %copy-start.3 = (f32[1,3,32,8,128]{4,3,2,1,0:T(8,128)S(1)}, f32[1,3,32,8,128]{4,3,2,1,0:T(8,128)}, u32[]{:S(2)}) copy-start(f32[1,3,32,8,128]{4,3,2,1,0:T(8,128)} %param.15) | copy-start | bytes 1179652
  17.6 1.0 copy-start
  19.0 0.7 copy-start.27
  20.0 1.0 copy-start.1
  21.1 11.2 %collective-permute-start.2 = (f32[3,32,1,128]{3,2,1,0:T(1,128)S(1)}, f32[3,32,1,128]{3,2,1,0:T(1,128)S(1)}, u32[]{:S(2)}, u32[]{:S(2)}) collective-permute-start(f32[3,32,1,128]{3,2,1,0:T(1,128)S(1)} %slice.655), channel_id=1, source_target_pairs={{0,1},{1,2},{2,3},{4,5},{5,6},{6,7},{8,9},{9,10},{10,11},{12,13},{... | collective-permute-start | bytes 147464 | tf_op jit(solution)/shard_map/ppermute | solution.py:15
  26.3 5.9 %collective-permute-start.3 = (f32[3,1,8,128]{3,2,1,0:T(8,128)S(1)}, f32[3,1,8,128]{3,2,1,0:T(8,128)S(1)}, u32[]{:S(2)}, u32[]{:S(2)}) collective-permute-start(f32[3,1,8,128]{3,2,1,0:T(8,128)S(1)} %slice.661), channel_id=1, source_target_pairs={{0,4},{1,5},{2,6},{3,7},{8,12},{9,13},{10,14},{11,15},{16,20},{17,... | collective-permute-start | bytes 36872 | tf_op jit(solution)/shard_map/ppermute | solution.py:15
  32.7 6.9 %collective-permute-start.4 = (f32[3,32,1,128]{3,2,1,0:T(1,128)S(1)}, f32[3,32,1,128]{3,2,1,0:T(1,128)S(1)}, u32[]{:S(2)}, u32[]{:S(2)}) collective-permute-start(f32[3,32,1,128]{3,2,1,0:T(1,128)S(1)} %slice.668), channel_id=1, source_target_pairs={{1,0},{2,1},{3,2},{5,4},{6,5},{7,6},{9,8},{10,9},{11,10},{13,12},{... | collective-permute-start | bytes 147464 | tf_op jit(solution)/shard_map/ppermute | solution.py:15
  34.0 5.6 %collective-permute-start.5 = (f32[3,1,8,128]{3,2,1,0:T(8,128)S(1)}, f32[3,1,8,128]{3,2,1,0:T(8,128)S(1)}, u32[]{:S(2)}, u32[]{:S(2)}) collective-permute-start(f32[3,1,8,128]{3,2,1,0:T(8,128)S(1)} %slice.674), channel_id=1, source_target_pairs={{4,0},{5,1},{6,2},{7,3},{12,8},{13,9},{14,10},{15,11},{20,16},{21,... | collective-permute-start | bytes 36872 | tf_op jit(solution)/shard_map/ppermute | solution.py:15
  39.8 7.4 %copy-start.2 = (f32[1,3,32,8,128]{4,3,2,1,0:T(8,128)S(1)}, f32[1,3,32,8,128]{4,3,2,1,0:T(8,128)}, u32[]{:S(2)}) copy-start(f32[1,3,32,8,128]{4,3,2,1,0:T(8,128)} %param.18) | copy-start | bytes 1179652
  40.0 12.7 %collective-permute-start.6 = (f32[3,32,1,128]{3,2,1,0:T(1,128)S(1)}, f32[3,32,1,128]{3,2,1,0:T(1,128)S(1)}, u32[]{:S(2)}, u32[]{:S(2)}) collective-permute-start(f32[3,32,1,128]{3,2,1,0:T(1,128)S(1)} %slice.678), channel_id=1, source_target_pairs={{0,1},{1,2},{2,3},{4,5},{5,6},{6,7},{8,9},{9,10},{10,11},{12,13},{... | collective-permute-start | bytes 147464 | tf_op jit(solution)/shard_map/ppermute | solution.py:15
  44.5 8.1 %collective-permute-start.7 = (f32[3,1,8,128]{3,2,1,0:T(8,128)S(1)}, f32[3,1,8,128]{3,2,1,0:T(8,128)S(1)}, u32[]{:S(2)}, u32[]{:S(2)}) collective-permute-start(f32[3,1,8,128]{3,2,1,0:T(8,128)S(1)} %slice.684), channel_id=1, source_target_pairs={{0,4},{1,5},{2,6},{3,7},{8,12},{9,13},{10,14},{11,15},{16,20},{17,... | collective-permute-start | bytes 36872 | tf_op jit(solution)/shard_map/ppermute | solution.py:15
  47.4 8.4 %collective-permute-start.14 = (f32[3,32,1,128]{3,2,1,0:T(1,128)S(1)}, f32[3,32,1,128]{3,2,1,0:T(1,128)S(1)}, u32[]{:S(2)}, u32[]{:S(2)}) collective-permute-start(f32[3,32,1,128]{3,2,1,0:T(1,128)S(1)} %slice.724), channel_id=1, source_target_pairs={{0,1},{1,2},{2,3},{4,5},{5,6},{6,7},{8,9},{9,10},{10,11},{12,13},{... | collective-permute-start | bytes 147464 | tf_op jit(solution)/shard_map/ppermute | solution.py:15
  51.3 4.5 %collective-permute-start.15 = (f32[3,1,8,128]{3,2,1,0:T(8,128)S(1)}, f32[3,1,8,128]{3,2,1,0:T(8,128)S(1)}, u32[]{:S(2)}, u32[]{:S(2)}) collective-permute-start(f32[3,1,8,128]{3,2,1,0:T(8,128)S(1)} %slice.730), channel_id=1, source_target_pairs={{0,4},{1,5},{2,6},{3,7},{8,12},{9,13},{10,14},{11,15},{16,20},{17,... | collective-permute-start | bytes 36872 | tf_op jit(solution)/shard_map/ppermute | solution.py:15
  53.1 6.9 %collective-permute-start.8 = (f32[3,32,1,128]{3,2,1,0:T(1,128)S(1)}, f32[3,32,1,128]{3,2,1,0:T(1,128)S(1)}, u32[]{:S(2)}, u32[]{:S(2)}) collective-permute-start(f32[3,32,1,128]{3,2,1,0:T(1,128)S(1)} %slice.691), channel_id=1, source_target_pairs={{1,0},{2,1},{3,2},{5,4},{6,5},{7,6},{9,8},{10,9},{11,10},{13,12},{... | collective-permute-start | bytes 147464 | tf_op jit(solution)/shard_map/ppermute | solution.py:15
  54.4 5.6 %collective-permute-start.9 = (f32[3,1,8,128]{3,2,1,0:T(8,128)S(1)}, f32[3,1,8,128]{3,2,1,0:T(8,128)S(1)}, u32[]{:S(2)}, u32[]{:S(2)}) collective-permute-start(f32[3,1,8,128]{3,2,1,0:T(8,128)S(1)} %slice.697), channel_id=1, source_target_pairs={{4,0},{5,1},{6,2},{7,3},{12,8},{13,9},{14,10},{15,11},{20,16},{21,... | collective-permute-start | bytes 36872 | tf_op jit(solution)/shard_map/ppermute | solution.py:15
  60.4 7.6 %collective-permute-start.10 = (f32[3,32,1,128]{3,2,1,0:T(1,128)S(1)}, f32[3,32,1,128]{3,2,1,0:T(1,128)S(1)}, u32[]{:S(2)}, u32[]{:S(2)}) collective-permute-start(f32[3,32,1,128]{3,2,1,0:T(1,128)S(1)} %slice.701), channel_id=1, source_target_pairs={{0,1},{1,2},{2,3},{4,5},{5,6},{6,7},{8,9},{9,10},{10,11},{12,13},{... | collective-permute-start | bytes 147464 | tf_op jit(solution)/shard_map/ppermute | solution.py:15
  64.9 3.0 %collective-permute-start.11 = (f32[3,1,8,128]{3,2,1,0:T(8,128)S(1)}, f32[3,1,8,128]{3,2,1,0:T(8,128)S(1)}, u32[]{:S(2)}, u32[]{:S(2)}) collective-permute-start(f32[3,1,8,128]{3,2,1,0:T(8,128)S(1)} %slice.707), channel_id=1, source_target_pairs={{0,4},{1,5},{2,6},{3,7},{8,12},{9,13},{10,14},{11,15},{16,20},{17,... | collective-permute-start | bytes 36872 | tf_op jit(solution)/shard_map/ppermute | solution.py:15
  68.5 0.8 copy-start.4
  69.3 15.5 %copy-start.17 = (f32[3,32,8]{2,1,0:T(8,128)}, f32[3,32,8]{2,1,0:T(8,128)S(1)}, u32[]{:S(2)}) copy-start(f32[3,32,8]{2,1,0:T(8,128)S(1)} %get-tuple-element.46) | copy-start | bytes 9220
  69.3 15.5 %copy-start.20 = (f32[3,32,8]{2,1,0:T(8,128)}, f32[3,32,8]{2,1,0:T(8,128)S(1)}, u32[]{:S(2)}) copy-start(f32[3,32,8]{2,1,0:T(8,128)S(1)} %get-tuple-element.45) | copy-start | bytes 9220
  69.5 6.9 %collective-permute-start.16 = (f32[3,32,1,128]{3,2,1,0:T(1,128)S(1)}, f32[3,32,1,128]{3,2,1,0:T(1,128)S(1)}, u32[]{:S(2)}, u32[]{:S(2)}) collective-permute-start(f32[3,32,1,128]{3,2,1,0:T(1,128)S(1)} %slice.736), channel_id=1, source_target_pairs={{1,0},{2,1},{3,2},{5,4},{6,5},{7,6},{9,8},{10,9},{11,10},{13,12},{... | collective-permute-start | bytes 147464 | tf_op jit(solution)/shard_map/ppermute | solution.py:15
  70.8 5.6 %collective-permute-start.17 = (f32[3,1,8,128]{3,2,1,0:T(8,128)S(1)}, f32[3,1,8,128]{3,2,1,0:T(8,128)S(1)}, u32[]{:S(2)}, u32[]{:S(2)}) collective-permute-start(f32[3,1,8,128]{3,2,1,0:T(8,128)S(1)} %slice.742), channel_id=1, source_target_pairs={{4,0},{5,1},{6,2},{7,3},{12,8},{13,9},{14,10},{15,11},{20,16},{21,... | collective-permute-start | bytes 36872 | tf_op jit(solution)/shard_map/ppermute | solution.py:15
  76.7 7.7 %copy-start.6 = (f32[1,32,8,128]{3,2,1,0:T(8,128)}, f32[1,32,8,128]{3,2,1,0:T(8,128)S(1)}, u32[]{:S(2)}) copy-start(f32[1,32,8,128]{3,2,1,0:T(8,128)S(1)} %get-tuple-element.67) | copy-start | bytes 393220
  76.9 7.6 %collective-permute-start.18 = (f32[3,32,1,128]{3,2,1,0:T(1,128)S(1)}, f32[3,32,1,128]{3,2,1,0:T(1,128)S(1)}, u32[]{:S(2)}, u32[]{:S(2)}) collective-permute-start(f32[3,32,1,128]{3,2,1,0:T(1,128)S(1)} %slice.746), channel_id=1, source_target_pairs={{0,1},{1,2},{2,3},{4,5},{5,6},{6,7},{8,9},{9,10},{10,11},{12,13},{... | collective-permute-start | bytes 147464 | tf_op jit(solution)/shard_map/ppermute | solution.py:15
  81.4 3.0 %collective-permute-start.19 = (f32[3,1,8,128]{3,2,1,0:T(8,128)S(1)}, f32[3,1,8,128]{3,2,1,0:T(8,128)S(1)}, u32[]{:S(2)}, u32[]{:S(2)}) collective-permute-start(f32[3,1,8,128]{3,2,1,0:T(8,128)S(1)} %slice.752), channel_id=1, source_target_pairs={{0,4},{1,5},{2,6},{3,7},{8,12},{9,13},{10,14},{11,15},{16,20},{17,... | collective-permute-start | bytes 36872 | tf_op jit(solution)/shard_map/ppermute | solution.py:15
  84.8 0.7 copy-start.8
  84.8 0.7 copy-start.11
  84.8 0.7 copy-start.14
  86.1 7.0 %collective-permute-start.20 = (f32[3,32,1,128]{3,2,1,0:T(1,128)}, f32[3,32,1,128]{3,2,1,0:T(1,128)}, u32[]{:S(2)}, u32[]{:S(2)}) collective-permute-start(f32[3,32,1,128]{3,2,1,0:T(1,128)} %slice.758), channel_id=1, source_target_pairs={{1,0},{2,1},{3,2},{5,4},{6,5},{7,6},{9,8},{10,9},{11,10},{13,12},{... | collective-permute-start | bytes 147464 | tf_op jit(solution)/shard_map/ppermute | solution.py:15
  87.4 5.7 %collective-permute-start.21 = (f32[3,1,8,128]{3,2,1,0:T(8,128)S(1)}, f32[3,1,8,128]{3,2,1,0:T(8,128)}, u32[]{:S(2)}, u32[]{:S(2)}) collective-permute-start(f32[3,1,8,128]{3,2,1,0:T(8,128)S(1)} %slice.764), channel_id=1, source_target_pairs={{4,0},{5,1},{6,2},{7,3},{12,8},{13,9},{14,10},{15,11},{20,16},{21,... | collective-permute-start | bytes 36872 | tf_op jit(solution)/shard_map/ppermute | solution.py:15
  90.3 2.8 %copy-start.9 = (f32[1,32,8,128]{3,2,1,0:T(8,128)S(1)}, f32[1,32,8,128]{3,2,1,0:T(8,128)}, u32[]{:S(2)}) copy-start(f32[1,32,8,128]{3,2,1,0:T(8,128)} %copy-done.8) | copy-start | bytes 393220
  90.3 2.8 %copy-start.12 = (f32[1,32,8,128]{3,2,1,0:T(8,128)S(1)}, f32[1,32,8,128]{3,2,1,0:T(8,128)}, u32[]{:S(2)}) copy-start(f32[1,32,8,128]{3,2,1,0:T(8,128)} %copy-done.11) | copy-start | bytes 393220
  90.3 2.8 %copy-start.15 = (f32[1,32,8,128]{3,2,1,0:T(8,128)S(1)}, f32[1,32,8,128]{3,2,1,0:T(8,128)}, u32[]{:S(2)}) copy-start(f32[1,32,8,128]{3,2,1,0:T(8,128)} %copy-done.14) | copy-start | bytes 393220
  90.3 2.8 %copy-start.18 = (f32[3,32,8]{2,1,0:T(8,128)S(1)}, f32[3,32,8]{2,1,0:T(8,128)}, u32[]{:S(2)}) copy-start(f32[3,32,8]{2,1,0:T(8,128)} %copy-done.17) | copy-start | bytes 9220
  90.3 2.8 %copy-start.21 = (f32[3,32,8]{2,1,0:T(8,128)S(1)}, f32[3,32,8]{2,1,0:T(8,128)}, u32[]{:S(2)}) copy-start(f32[3,32,8]{2,1,0:T(8,128)} %copy-done.20) | copy-start | bytes 9220
  94.3 0.9 copy-start.7
  95.2 8.0 %copy-start.5 = (f32[3,32,8,128]{3,2,1,0:T(8,128)S(1)}, f32[3,32,8,128]{3,2,1,0:T(8,128)}, u32[]{:S(2)}) copy-start(f32[3,32,8,128]{3,2,1,0:T(8,128)} %copy-done.4) | copy-start | bytes 1179652
  95.4 9.2 %collective-permute-start.22 = (f32[3,32,1,128]{3,2,1,0:T(1,128)S(1)}, f32[3,32,1,128]{3,2,1,0:T(1,128)S(1)}, u32[]{:S(2)}, u32[]{:S(2)}) collective-permute-start(f32[3,32,1,128]{3,2,1,0:T(1,128)S(1)} %slice.768), channel_id=1, source_target_pairs={{0,1},{1,2},{2,3},{4,5},{5,6},{6,7},{8,9},{9,10},{10,11},{12,13},{... | collective-permute-start | bytes 147464 | tf_op jit(solution)/shard_map/ppermute | solution.py:15
  100.0 4.7 %collective-permute-start.23 = (f32[3,1,8,128]{3,2,1,0:T(8,128)S(1)}, f32[3,1,8,128]{3,2,1,0:T(8,128)S(1)}, u32[]{:S(2)}, u32[]{:S(2)}) collective-permute-start(f32[3,1,8,128]{3,2,1,0:T(8,128)S(1)} %slice.774), channel_id=1, source_target_pairs={{0,4},{1,5},{2,6},{3,7},{8,12},{9,13},{10,14},{11,15},{16,20},{17,... | collective-permute-start | bytes 36872 | tf_op jit(solution)/shard_map/ppermute | solution.py:15
  104.9 0.9 copy-start.23
  104.9 0.9 copy-start.25
  105.0 0.8 copy-start.28
  106.5 12.5 %copy-start.19 = (f32[3,32,8]{2,1,0:T(8,128)S(1)}, f32[3,32,8]{2,1,0:T(8,128)}, u32[]{:S(2)}) copy-start(f32[3,32,8]{2,1,0:T(8,128)} %copy-done.17) | copy-start | bytes 9220
  106.5 12.5 %copy-start.22 = (f32[3,32,8]{2,1,0:T(8,128)S(1)}, f32[3,32,8]{2,1,0:T(8,128)}, u32[]{:S(2)}) copy-start(f32[3,32,8]{2,1,0:T(8,128)} %copy-done.20) | copy-start | bytes 9220
  118.1 0.9 copy-start.13
  118.1 1.0 copy-start.16
  118.2 0.9 copy-start.10
where the time goes:
time: 121 us; the launch traced here: 120 us
  starting transfers between devices  58 us (48%)
  waiting for transfers between devices  19.5 us (16%)
  blocking collectives  17.8 us (15%)
  local copies, waits for them, and re-layouts  13.3 us (11%)
  other arithmetic  8.24 us (7%)
  between operations  3.44 us (3%)
    ppermute x24, starting transfers between devices, shifted_2(): return lax.ppermute(block, axis, route)  58 us
    ppermute x24, waiting for transfers between devices, shifted_2(): return lax.ppermute(block, axis, route)  19.5 us
    psum x1, blocking collectives, per_device(): summed = lax.psum(local_grad, 'wl')  11.6 us
    all_gather x1, blocking collectives, per_device(): tiles = lax.all_gather(design, 'wl', axis=0, tiled=True)  6.17 us
    unnamed x59, local copies, waits for them, and re-layouts  5.58 us
    slice x12, local copies, waits for them, and re-layouts, neighbours(): plane_y = stacked[:, :, :1] if upward else stacked[:, :, -1:]  3.04 us
  transfers between devices with their start and end apart: 24, of which 8 were waited for; matrix products, arithmetic and copies ran while one was open for 6% of the time, Pallas kernels for 0%

commit v1 on v0

--- a/solution.py
+++ b/solution.py
@@ -7,6 +7,16 @@
 Z0 = 64
 STEPS = 3
 time_step = 0.5
+
+
+def gather_by_hops(x, axis, dim):
+    size = lax.axis_size(axis)
+    held, tiles = (x, [x])
+    for _ in range(size - 1):
+        held = lax.ppermute(held, axis, [(i, (i + 1) % size) for i in range(size)])
+        tiles.insert(0, held)
+    row_of_blocks = jnp.concatenate(tiles, axis=dim)
+    return jnp.roll(row_of_blocks, (lax.axis_index(axis) + 1) * x.shape[dim], axis=dim)
 
 
 def shifted_2(block, axis, distance):
@@ -80,7 +90,7 @@
     owned = design.shape[0]
     slab_depth = owned * groups
     depth = background.shape[2]
-    tiles = lax.all_gather(design, "wl", axis=0, tiled=True)
+    tiles = gather_by_hops(design, "wl", 0)
     permit = jnp.concatenate(
         [
             background[:, :, :Z0],

time: 121 us -> 125 us (1.033)
  blocking collectives: 17.8 us -> 11.7 us
  local copies, waits for them, and re-layouts: 13.3 us -> 17.5 us
  starting transfers between devices: 58 us -> 60.9 us
  other arithmetic: 8.24 us -> 10.8 us
    all_gather x1 -> x0, blocking collectives: 6.17 us -> none  [per_device(): tiles = lax.all_gather(design, 'wl', axis=0, tiled=True)]
    ppermute x0 -> x3, starting transfers between devices: none -> 3.23 us  [gather_by_hops(): held = lax.ppermute(held, axis, [(i, (i + 1) % size) for i in range(size)])]
    sub x6, other arithmetic: 1.96 us -> 3.58 us  [along(): return shifted - stacked]
    unnamed x59 -> x64, local copies, waits for them, and re-layouts: 5.58 us -> 6.26 us
  transfers between devices with their start and end apart: 24 -> 27, of which waited for: 8 -> 8; matrix products, arithmetic and copies ran while one was open for 6% -> 10% of each run, Pallas kernels for 0% -> 0%
where the time goes in v1:
time: 125 us; the launch traced here: 124 us
  starting transfers between devices  60.9 us (49%)
  waiting for transfers between devices  19.4 us (16%)
  local copies, waits for them, and re-layouts  17.5 us (14%)
  blocking collectives  11.7 us (9%)
  other arithmetic  10.8 us (9%)
  between operations  3.47 us (3%)
    ppermute x24, starting transfers between devices, shifted_2(): return lax.ppermute(block, axis, route)  57.7 us
    ppermute x24, waiting for transfers between devices, shifted_2(): return lax.ppermute(block, axis, route)  19.4 us
    psum x1, blocking collectives, per_device(): summed = lax.psum(local_grad, 'wl')  11.7 us
    unnamed x64, local copies, waits for them, and re-layouts  6.26 us
    slice x12, local copies, waits for them, and re-layouts, neighbours(): plane_y = stacked[:, :, :1] if upward else stacked[:, :, -1:]  4.28 us
    sub x6, other arithmetic, along(): return shifted - stacked  3.58 us
    ppermute x3, starting transfers between devices, gather_by_hops(): held = lax.ppermute(held, axis, [(i, (i + 1) % size) for i in range(size)])  3.23 us
    slice x12, local copies, waits for them, and re-layouts, neighbours(): plane_x = stacked[:, :1] if upward else stacked[:, -1:]  2.65 us
  transfers between devices with their start and end apart: 27, of which 8 were waited for; matrix products, arithmetic and copies ran while one was open for 10% of the time, Pallas kernels for 0%

profile of v1, /device:TPU:0, one launch (start us, length us, event | category | flops | bytes accessed | tf_op | source)
XLA Modules:
  0.0 123.8 jit_solution(17234926804471576149)
XLA Ops:
  0.6 1.6 %slice.645 = f32[3,32,1,128]{3,2,1,0:T(1,128)} slice(f32[3,32,8,128]{3,2,1,0:T(8,128)} %bitcast.77), slice={[0:3], [0:32], [0:1], [0:128]} | slice | bytes 98304 | tf_op jit(solution)/shard_map/slice | solution.py:31
  2.3 1.4 %collective-permute-start.3 = (f32[3,32,1,128]{3,2,1,0:T(1,128)}, f32[3,32,1,128]{3,2,1,0:T(1,128)}, u32[]{:S(2)}, u32[]{:S(2)}) collective-permute-start(f32[3,32,1,128]{3,2,1,0:T(1,128)} %slice.645), channel_id=1, source_target_pairs={{1,0},{2,1},{3,2},{5,4},{6,5},{7,6},{9,8},{10,9},{11,10},{13,12},{... | collective-permute-start | bytes 147464 | tf_op jit(solution)/shard_map/ppermute | solution.py:25
  3.7 1.3 %slice.651 = f32[3,1,8,128]{3,2,1,0:T(8,128)} slice(f32[3,32,8,128]{3,2,1,0:T(8,128)} %bitcast.78), slice={[0:3], [0:1], [0:8], [0:128]} | slice | bytes 24576 | tf_op jit(solution)/shard_map/slice | solution.py:30
  5.0 1.3 %collective-permute-start.4 = (f32[3,1,8,128]{3,2,1,0:T(8,128)}, f32[3,1,8,128]{3,2,1,0:T(8,128)}, u32[]{:S(2)}, u32[]{:S(2)}) collective-permute-start(f32[3,1,8,128]{3,2,1,0:T(8,128)} %slice.651), channel_id=1, source_target_pairs={{4,0},{5,1},{6,2},{7,3},{12,8},{13,9},{14,10},{15,11},{20,16},{21,... | collective-permute-start | bytes 36872 | tf_op jit(solution)/shard_map/ppermute | solution.py:25
  6.3 0.5 collective-permute-start
  6.8 1.6 %slice.714 = f32[3,32,1,128]{3,2,1,0:T(1,128)} slice(f32[3,32,8,128]{3,2,1,0:T(8,128)} %bitcast.72), slice={[0:3], [0:32], [0:1], [0:128]} | slice | bytes 98304 | tf_op jit(solution)/shard_map/slice | solution.py:31
  8.4 1.3 %collective-permute-start.15 = (f32[3,32,1,128]{3,2,1,0:T(1,128)}, f32[3,32,1,128]{3,2,1,0:T(1,128)}, u32[]{:S(2)}, u32[]{:S(2)}) collective-permute-start(f32[3,32,1,128]{3,2,1,0:T(1,128)} %slice.714), channel_id=1, source_target_pairs={{1,0},{2,1},{3,2},{5,4},{6,5},{7,6},{9,8},{10,9},{11,10},{13,12},{... | collective-permute-start | bytes 147464 | tf_op jit(solution)/shard_map/ppermute | solution.py:25
  9.7 1.3 %slice.720 = f32[3,1,8,128]{3,2,1,0:T(8,128)} slice(f32[3,32,8,128]{3,2,1,0:T(8,128)} %bitcast.73), slice={[0:3], [0:1], [0:8], [0:128]} | slice | bytes 24576 | tf_op jit(solution)/shard_map/slice | solution.py:30
  11.0 1.3 %collective-permute-start.16 = (f32[3,1,8,128]{3,2,1,0:T(8,128)}, f32[3,1,8,128]{3,2,1,0:T(8,128)S(1)}, u32[]{:S(2)}, u32[]{:S(2)}) collective-permute-start(f32[3,1,8,128]{3,2,1,0:T(8,128)} %slice.720), channel_id=1, source_target_pairs={{4,0},{5,1},{6,2},{7,3},{12,8},{13,9},{14,10},{15,11},{20,16},{21,... | collective-permute-start | bytes 36872 | tf_op jit(solution)/shard_map/ppermute | solution.py:25
  13.6 2.7 %collective-permute-start.1 = (f32[2,32,8]{1,2,0:T(8,128)S(1)}, f32[2,32,8]{1,2,0:T(8,128)S(1)}, u32[]{:S(2)}, u32[]{:S(2)}) collective-permute-start(f32[2,32,8]{1,2,0:T(8,128)S(1)} %collective-permute-done), channel_id=1, source_target_pairs={{0,8},{8,16},{16,24},{24,0},{1,9},{9,17},{17,25},{25,1},{2,10},{10... | collective-permute-start | bytes 6152 | tf_op jit(solution)/shard_map/ppermute | solution.py:16
  16.3 1.1 slice.644
  17.7 0.9 copy-done
  18.9 0.8 copy-done.23
  19.7 0.8 slice.502
  20.7 0.6 copy-done.26
  21.7 1.1 maximum_divide_fusion
  22.8 0.9 pad_subtract_fusion.11
  23.8 0.9 copy-done.1
  24.8 5.2 %collective-permute-start.5 = (f32[3,32,1,128]{3,2,1,0:T(1,128)S(1)}, f32[3,32,1,128]{3,2,1,0:T(1,128)S(1)}, u32[]{:S(2)}, u32[]{:S(2)}) collective-permute-start(f32[3,32,1,128]{3,2,1,0:T(1,128)S(1)} %slice.655), channel_id=1, source_target_pairs={{0,1},{1,2},{2,3},{4,5},{5,6},{6,7},{8,9},{9,10},{10,11},{12,13},{... | collective-permute-start | bytes 147464 | tf_op jit(solution)/shard_map/ppermute | solution.py:25
  30.0 5.1 %collective-permute-start.6 = (f32[3,1,8,128]{3,2,1,0:T(8,128)S(1)}, f32[3,1,8,128]{3,2,1,0:T(8,128)S(1)}, u32[]{:S(2)}, u32[]{:S(2)}) collective-permute-start(f32[3,1,8,128]{3,2,1,0:T(8,128)S(1)} %slice.661), channel_id=1, source_target_pairs={{0,4},{1,5},{2,6},{3,7},{8,12},{9,13},{10,14},{11,15},{16,20},{17,... | collective-permute-start | bytes 36872 | tf_op jit(solution)/shard_map/ppermute | solution.py:25
  35.1 1.0 pad_subtract_fusion.5
  36.1 0.4 collective-permute-done.6
  37.0 1.3 %collective-permute-start.7 = (f32[3,32,1,128]{3,2,1,0:T(1,128)S(1)}, f32[3,32,1,128]{3,2,1,0:T(1,128)S(1)}, u32[]{:S(2)}, u32[]{:S(2)}) collective-permute-start(f32[3,32,1,128]{3,2,1,0:T(1,128)S(1)} %slice.668), channel_id=1, source_target_pairs={{1,0},{2,1},{3,2},{5,4},{6,5},{7,6},{9,8},{10,9},{11,10},{13,12},{... | collective-permute-start | bytes 147464 | tf_op jit(solution)/shard_map/ppermute | solution.py:25
  38.3 1.3 %collective-permute-start.8 = (f32[3,1,8,128]{3,2,1,0:T(8,128)S(1)}, f32[3,1,8,128]{3,2,1,0:T(8,128)S(1)}, u32[]{:S(2)}, u32[]{:S(2)}) collective-permute-start(f32[3,1,8,128]{3,2,1,0:T(8,128)S(1)} %slice.674), channel_id=1, source_target_pairs={{4,0},{5,1},{6,2},{7,3},{12,8},{13,9},{14,10},{15,11},{20,16},{21,... | collective-permute-start | bytes 36872 | tf_op jit(solution)/shard_map/ppermute | solution.py:25
  39.9 4.0 %collective-permute-done.8 = f32[3,1,8,128]{3,2,1,0:T(8,128)S(1)} collective-permute-done((f32[3,1,8,128]{3,2,1,0:T(8,128)S(1)}, f32[3,1,8,128]{3,2,1,0:T(8,128)S(1)}, u32[]{:S(2)}, u32[]{:S(2)}) %collective-permute-start.8) | collective-permute-done | bytes 12320 | tf_op jit(solution)/shard_map/ppermute | solution.py:25
  44.2 4.5 %collective-permute-start.9 = (f32[3,32,1,128]{3,2,1,0:T(1,128)S(1)}, f32[3,32,1,128]{3,2,1,0:T(1,128)S(1)}, u32[]{:S(2)}, u32[]{:S(2)}) collective-permute-start(f32[3,32,1,128]{3,2,1,0:T(1,128)S(1)} %slice.678), channel_id=1, source_target_pairs={{0,1},{1,2},{2,3},{4,5},{5,6},{6,7},{8,9},{9,10},{10,11},{12,13},{... | collective-permute-start | bytes 147464 | tf_op jit(solution)/shard_map/ppermute | solution.py:25
  48.8 2.5 %collective-permute-start.10 = (f32[3,1,8,128]{3,2,1,0:T(8,128)S(1)}, f32[3,1,8,128]{3,2,1,0:T(8,128)S(1)}, u32[]{:S(2)}, u32[]{:S(2)}) collective-permute-start(f32[3,1,8,128]{3,2,1,0:T(8,128)S(1)} %slice.684), channel_id=1, source_target_pairs={{0,4},{1,5},{2,6},{3,7},{8,12},{9,13},{10,14},{11,15},{16,20},{17,... | collective-permute-start | bytes 36872 | tf_op jit(solution)/shard_map/ppermute | solution.py:25
  51.5 3.9 %collective-permute-start.17 = (f32[3,32,1,128]{3,2,1,0:T(1,128)S(1)}, f32[3,32,1,128]{3,2,1,0:T(1,128)S(1)}, u32[]{:S(2)}, u32[]{:S(2)}) collective-permute-start(f32[3,32,1,128]{3,2,1,0:T(1,128)S(1)} %slice.724), channel_id=1, source_target_pairs={{0,1},{1,2},{2,3},{4,5},{5,6},{6,7},{8,9},{9,10},{10,11},{12,13},{... | collective-permute-start | bytes 147464 | tf_op jit(solution)/shard_map/ppermute | solution.py:25
  55.4 1.3 %collective-permute-start.18 = (f32[3,1,8,128]{3,2,1,0:T(8,128)S(1)}, f32[3,1,8,128]{3,2,1,0:T(8,128)S(1)}, u32[]{:S(2)}, u32[]{:S(2)}) collective-permute-start(f32[3,1,8,128]{3,2,1,0:T(8,128)S(1)} %slice.730), channel_id=1, source_target_pairs={{0,4},{1,5},{2,6},{3,7},{8,12},{9,13},{10,14},{11,15},{16,20},{17,... | collective-permute-start | bytes 36872 | tf_op jit(solution)/shard_map/ppermute | solution.py:25
  56.8 0.2 pad_subtract_fusion.8
  57.3 1.3 %collective-permute-start.11 = (f32[3,32,1,128]{3,2,1,0:T(1,128)S(1)}, f32[3,32,1,128]{3,2,1,0:T(1,128)S(1)}, u32[]{:S(2)}, u32[]{:S(2)}) collective-permute-start(f32[3,32,1,128]{3,2,1,0:T(1,128)S(1)} %slice.691), channel_id=1, source_target_pairs={{1,0},{2,1},{3,2},{5,4},{6,5},{7,6},{9,8},{10,9},{11,10},{13,12},{... | collective-permute-start | bytes 147464 | tf_op jit(solution)/shard_map/ppermute | solution.py:25
  58.6 1.3 %collective-permute-start.12 = (f32[3,1,8,128]{3,2,1,0:T(8,128)S(1)}, f32[3,1,8,128]{3,2,1,0:T(8,128)S(1)}, u32[]{:S(2)}, u32[]{:S(2)}) collective-permute-start(f32[3,1,8,128]{3,2,1,0:T(8,128)S(1)} %slice.697), channel_id=1, source_target_pairs={{4,0},{5,1},{6,2},{7,3},{12,8},{13,9},{14,10},{15,11},{20,16},{21,... | collective-permute-start | bytes 36872 | tf_op jit(solution)/shard_map/ppermute | solution.py:25
  60.4 3.8 %collective-permute-done.12 = f32[3,1,8,128]{3,2,1,0:T(8,128)S(1)} collective-permute-done((f32[3,1,8,128]{3,2,1,0:T(8,128)S(1)}, f32[3,1,8,128]{3,2,1,0:T(8,128)S(1)}, u32[]{:S(2)}, u32[]{:S(2)}) %collective-permute-start.12) | collective-permute-done | bytes 12320 | tf_op jit(solution)/shard_map/ppermute | solution.py:25
  64.5 4.5 %collective-permute-start.13 = (f32[3,32,1,128]{3,2,1,0:T(1,128)S(1)}, f32[3,32,1,128]{3,2,1,0:T(1,128)S(1)}, u32[]{:S(2)}, u32[]{:S(2)}) collective-permute-start(f32[3,32,1,128]{3,2,1,0:T(1,128)S(1)} %slice.701), channel_id=1, source_target_pairs={{0,1},{1,2},{2,3},{4,5},{5,6},{6,7},{8,9},{9,10},{10,11},{12,13},{... | collective-permute-start | bytes 147464 | tf_op jit(solution)/shard_map/ppermute | solution.py:25
  69.1 1.6 %collective-permute-start.14 = (f32[3,1,8,128]{3,2,1,0:T(8,128)S(1)}, f32[3,1,8,128]{3,2,1,0:T(8,128)S(1)}, u32[]{:S(2)}, u32[]{:S(2)}) collective-permute-start(f32[3,1,8,128]{3,2,1,0:T(8,128)S(1)} %slice.707), channel_id=1, source_target_pairs={{0,4},{1,5},{2,6},{3,7},{8,12},{9,13},{10,14},{11,15},{16,20},{17,... | collective-permute-start | bytes 36872 | tf_op jit(solution)/shard_map/ppermute | solution.py:25
  70.8 1.3 %collective-permute-done.14 = f32[3,1,8,128]{3,2,1,0:T(8,128)S(1)} collective-permute-done((f32[3,1,8,128]{3,2,1,0:T(8,128)S(1)}, f32[3,1,8,128]{3,2,1,0:T(8,128)S(1)}, u32[]{:S(2)}, u32[]{:S(2)}) %collective-permute-start.14) | collective-permute-done | bytes 12320 | tf_op jit(solution)/shard_map/ppermute | solution.py:25
  72.1 0.2 pad_subtract_fusion.6
  72.6 0.8 multiply_reduce_fusion
  73.7 1.3 %collective-permute-start.19 = (f32[3,32,1,128]{3,2,1,0:T(1,128)S(1)}, f32[3,32,1,128]{3,2,1,0:T(1,128)S(1)}, u32[]{:S(2)}, u32[]{:S(2)}) collective-permute-start(f32[3,32,1,128]{3,2,1,0:T(1,128)S(1)} %slice.736), channel_id=1, source_target_pairs={{1,0},{2,1},{3,2},{5,4},{6,5},{7,6},{9,8},{10,9},{11,10},{13,12},{... | collective-permute-start | bytes 147464 | tf_op jit(solution)/shard_map/ppermute | solution.py:25
  75.0 1.3 %collective-permute-start.20 = (f32[3,1,8,128]{3,2,1,0:T(8,128)S(1)}, f32[3,1,8,128]{3,2,1,0:T(8,128)S(1)}, u32[]{:S(2)}, u32[]{:S(2)}) collective-permute-start(f32[3,1,8,128]{3,2,1,0:T(8,128)S(1)} %slice.742), channel_id=1, source_target_pairs={{4,0},{5,1},{6,2},{7,3},{12,8},{13,9},{14,10},{15,11},{20,16},{21,... | collective-permute-start | bytes 36872 | tf_op jit(solution)/shard_map/ppermute | solution.py:25
  76.5 4.0 %collective-permute-done.20 = f32[3,1,8,128]{3,2,1,0:T(8,128)S(1)} collective-permute-done((f32[3,1,8,128]{3,2,1,0:T(8,128)S(1)}, f32[3,1,8,128]{3,2,1,0:T(8,128)S(1)}, u32[]{:S(2)}, u32[]{:S(2)}) %collective-permute-start.20) | collective-permute-done | bytes 12320 | tf_op jit(solution)/shard_map/ppermute | solution.py:25
  80.6 0.3 pad_subtract_fusion.3
  81.0 4.5 %collective-permute-start.21 = (f32[3,32,1,128]{3,2,1,0:T(1,128)S(1)}, f32[3,32,1,128]{3,2,1,0:T(1,128)S(1)}, u32[]{:S(2)}, u32[]{:S(2)}) collective-permute-start(f32[3,32,1,128]{3,2,1,0:T(1,128)S(1)} %slice.746), channel_id=1, source_target_pairs={{0,1},{1,2},{2,3},{4,5},{5,6},{6,7},{8,9},{9,10},{10,11},{12,13},{... | collective-permute-start | bytes 147464 | tf_op jit(solution)/shard_map/ppermute | solution.py:25
  85.6 1.6 %collective-permute-start.22 = (f32[3,1,8,128]{3,2,1,0:T(8,128)S(1)}, f32[3,1,8,128]{3,2,1,0:T(8,128)S(1)}, u32[]{:S(2)}, u32[]{:S(2)}) collective-permute-start(f32[3,1,8,128]{3,2,1,0:T(8,128)S(1)} %slice.752), channel_id=1, source_target_pairs={{0,4},{1,5},{2,6},{3,7},{8,12},{9,13},{10,14},{11,15},{16,20},{17,... | collective-permute-start | bytes 36872 | tf_op jit(solution)/shard_map/ppermute | solution.py:25
  87.3 1.4 %collective-permute-done.22 = f32[3,1,8,128]{3,2,1,0:T(8,128)S(1)} collective-permute-done((f32[3,1,8,128]{3,2,1,0:T(8,128)S(1)}, f32[3,1,8,128]{3,2,1,0:T(8,128)S(1)}, u32[]{:S(2)}, u32[]{:S(2)}) %collective-permute-start.22) | collective-permute-done | bytes 12320 | tf_op jit(solution)/shard_map/ppermute | solution.py:25
  88.9 0.3 fusion.24
  89.2 0.3 copy-done.8
  89.6 0.6 slice.758
  90.3 1.3 %collective-permute-start.23 = (f32[3,32,1,128]{3,2,1,0:T(1,128)}, f32[3,32,1,128]{3,2,1,0:T(1,128)}, u32[]{:S(2)}, u32[]{:S(2)}) collective-permute-start(f32[3,32,1,128]{3,2,1,0:T(1,128)} %slice.758), channel_id=1, source_target_pairs={{1,0},{2,1},{3,2},{5,4},{6,5},{7,6},{9,8},{10,9},{11,10},{13,12},{... | collective-permute-start | bytes 147464 | tf_op jit(solution)/shard_map/ppermute | solution.py:25
  91.6 1.3 %collective-permute-start.24 = (f32[3,1,8,128]{3,2,1,0:T(8,128)S(1)}, f32[3,1,8,128]{3,2,1,0:T(8,128)}, u32[]{:S(2)}, u32[]{:S(2)}) collective-permute-start(f32[3,1,8,128]{3,2,1,0:T(8,128)S(1)} %slice.764), channel_id=1, source_target_pairs={{4,0},{5,1},{6,2},{7,3},{12,8},{13,9},{14,10},{15,11},{20,16},{21,... | collective-permute-start | bytes 36872 | tf_op jit(solution)/shard_map/ppermute | solution.py:25
  92.9 0.6 slice.786
  93.8 3.4 %collective-permute-done.24 = f32[3,1,8,128]{3,2,1,0:T(8,128)} collective-permute-done((f32[3,1,8,128]{3,2,1,0:T(8,128)S(1)}, f32[3,1,8,128]{3,2,1,0:T(8,128)}, u32[]{:S(2)}, u32[]{:S(2)}) %collective-permute-start.24) | collective-permute-done | bytes 12320 | tf_op jit(solution)/shard_map/ppermute | solution.py:25
  97.3 1.2 pad_subtract_fusion.1
  98.5 0.8 copy-done.7
  99.5 4.5 %collective-permute-start.25 = (f32[3,32,1,128]{3,2,1,0:T(1,128)S(1)}, f32[3,32,1,128]{3,2,1,0:T(1,128)S(1)}, u32[]{:S(2)}, u32[]{:S(2)}) collective-permute-start(f32[3,32,1,128]{3,2,1,0:T(1,128)S(1)} %slice.768), channel_id=1, source_target_pairs={{0,1},{1,2},{2,3},{4,5},{5,6},{6,7},{8,9},{9,10},{10,11},{12,13},{... | collective-permute-start | bytes 147464 | tf_op jit(solution)/shard_map/ppermute | solution.py:25
  104.1 2.6 %collective-permute-start.26 = (f32[3,1,8,128]{3,2,1,0:T(8,128)S(1)}, f32[3,1,8,128]{3,2,1,0:T(8,128)S(1)}, u32[]{:S(2)}, u32[]{:S(2)}) collective-permute-start(f32[3,1,8,128]{3,2,1,0:T(8,128)S(1)} %slice.774), channel_id=1, source_target_pairs={{0,4},{1,5},{2,6},{3,7},{8,12},{9,13},{10,14},{11,15},{16,20},{17,... | collective-permute-start | bytes 36872 | tf_op jit(solution)/shard_map/ppermute | solution.py:25
  106.7 0.3 fusion.6
  107.1 1.1 collective-permute-done.26
  108.1 0.3 pad_subtract_fusion
  108.5 0.7 copy-done.24
  109.2 0.6 fusion.5
  109.8 11.7 %psum.7 = f32[8,32,8]{0,2,1:T(8,128)S(1)} all-reduce(f32[8,32,8]{0,2,1:T(8,128)S(1)} %multiply_bitcast_fusion), channel_id=1, replica_groups=mesh['wl'=4,'gx'=2,'gy'=4] {'wl'}, use_global_device_ids=true, to_apply=%region_6.7 | all-reduce | flops 2048 | bytes 16384 | tf_op jit(solution)/shard_map/psum | solution.py:121
  121.7 0.7 copy.16
  122.6 1.1 fusion.19
  (157 shorter events, 5.4 us)
Async XLA Ops:
  2.3 4.0 %copy-start.25 = (f32[2,32,8]{1,2,0:T(8,128)S(1)}, f32[2,32,8]{1,2,0:T(8,128)}, u32[]{:S(2)}) copy-start(f32[2,32,8]{1,2,0:T(8,128)} %param.20) | copy-start | bytes 6148
  2.3 20.5 %collective-permute-start.3 = (f32[3,32,1,128]{3,2,1,0:T(1,128)}, f32[3,32,1,128]{3,2,1,0:T(1,128)}, u32[]{:S(2)}, u32[]{:S(2)}) collective-permute-start(f32[3,32,1,128]{3,2,1,0:T(1,128)} %slice.645), channel_id=1, source_target_pairs={{1,0},{2,1},{3,2},{5,4},{6,5},{7,6},{9,8},{10,9},{11,10},{13,12},{... | collective-permute-start | bytes 147464 | tf_op jit(solution)/shard_map/ppermute | solution.py:25
  5.0 17.7 %collective-permute-start.4 = (f32[3,1,8,128]{3,2,1,0:T(8,128)}, f32[3,1,8,128]{3,2,1,0:T(8,128)}, u32[]{:S(2)}, u32[]{:S(2)}) collective-permute-start(f32[3,1,8,128]{3,2,1,0:T(8,128)} %slice.651), channel_id=1, source_target_pairs={{4,0},{5,1},{6,2},{7,3},{12,8},{13,9},{14,10},{15,11},{20,16},{21,... | collective-permute-start | bytes 36872 | tf_op jit(solution)/shard_map/ppermute | solution.py:25
  6.3 7.3 %collective-permute-start = (f32[2,32,8]{1,2,0:T(8,128)S(1)}, f32[2,32,8]{1,2,0:T(8,128)S(1)}, u32[]{:S(2)}, u32[]{:S(2)}) collective-permute-start(f32[2,32,8]{1,2,0:T(8,128)S(1)} %copy-done.25), channel_id=1, source_target_pairs={{0,8},{8,16},{16,24},{24,0},{1,9},{9,17},{17,25},{25,1},{2,10},{10... | collective-permute-start | bytes 6152 | tf_op jit(solution)/shard_map/ppermute | solution.py:16
  8.4 26.6 %collective-permute-start.15 = (f32[3,32,1,128]{3,2,1,0:T(1,128)}, f32[3,32,1,128]{3,2,1,0:T(1,128)}, u32[]{:S(2)}, u32[]{:S(2)}) collective-permute-start(f32[3,32,1,128]{3,2,1,0:T(1,128)} %slice.714), channel_id=1, source_target_pairs={{1,0},{2,1},{3,2},{5,4},{6,5},{7,6},{9,8},{10,9},{11,10},{13,12},{... | collective-permute-start | bytes 147464 | tf_op jit(solution)/shard_map/ppermute | solution.py:25
  11.0 24.0 %collective-permute-start.16 = (f32[3,1,8,128]{3,2,1,0:T(8,128)}, f32[3,1,8,128]{3,2,1,0:T(8,128)S(1)}, u32[]{:S(2)}, u32[]{:S(2)}) collective-permute-start(f32[3,1,8,128]{3,2,1,0:T(8,128)} %slice.720), channel_id=1, source_target_pairs={{4,0},{5,1},{6,2},{7,3},{12,8},{13,9},{14,10},{15,11},{20,16},{21,... | collective-permute-start | bytes 36872 | tf_op jit(solution)/shard_map/ppermute | solution.py:25
  13.6 4.0 %collective-permute-start.1 = (f32[2,32,8]{1,2,0:T(8,128)S(1)}, f32[2,32,8]{1,2,0:T(8,128)S(1)}, u32[]{:S(2)}, u32[]{:S(2)}) collective-permute-start(f32[2,32,8]{1,2,0:T(8,128)S(1)} %collective-permute-done), channel_id=1, source_target_pairs={{0,8},{8,16},{16,24},{24,0},{1,9},{9,17},{17,25},{25,1},{2,10},{10... | collective-permute-start | bytes 6152 | tf_op jit(solution)/shard_map/ppermute | solution.py:16
  16.3 1.1 copy-start.3
  17.6 1.0 copy-start
  17.6 3.8 %collective-permute-start.2 = (f32[2,32,8]{1,2,0:T(8,128)S(1)}, f32[2,32,8]{1,2,0:T(8,128)S(1)}, u32[]{:S(2)}, u32[]{:S(2)}) collective-permute-start(f32[2,32,8]{1,2,0:T(8,128)S(1)} %collective-permute-done.1), channel_id=1, source_target_pairs={{0,8},{8,16},{16,24},{24,0},{1,9},{9,17},{17,25},{25,1},{2,10},{10... | collective-permute-start | bytes 6152 | tf_op jit(solution)/shard_map/ppermute | solution.py:16
  18.8 0.9 copy-start.23
  20.6 0.7 copy-start.26
  23.7 1.0 copy-start.1
  24.8 11.7 %collective-permute-start.5 = (f32[3,32,1,128]{3,2,1,0:T(1,128)S(1)}, f32[3,32,1,128]{3,2,1,0:T(1,128)S(1)}, u32[]{:S(2)}, u32[]{:S(2)}) collective-permute-start(f32[3,32,1,128]{3,2,1,0:T(1,128)S(1)} %slice.655), channel_id=1, source_target_pairs={{0,1},{1,2},{2,3},{4,5},{5,6},{6,7},{8,9},{9,10},{10,11},{12,13},{... | collective-permute-start | bytes 147464 | tf_op jit(solution)/shard_map/ppermute | solution.py:25
  30.0 6.5 %collective-permute-start.6 = (f32[3,1,8,128]{3,2,1,0:T(8,128)S(1)}, f32[3,1,8,128]{3,2,1,0:T(8,128)S(1)}, u32[]{:S(2)}, u32[]{:S(2)}) collective-permute-start(f32[3,1,8,128]{3,2,1,0:T(8,128)S(1)} %slice.661), channel_id=1, source_target_pairs={{0,4},{1,5},{2,6},{3,7},{8,12},{9,13},{10,14},{11,15},{16,20},{17,... | collective-permute-start | bytes 36872 | tf_op jit(solution)/shard_map/ppermute | solution.py:25
  37.0 6.9 %collective-permute-start.7 = (f32[3,32,1,128]{3,2,1,0:T(1,128)S(1)}, f32[3,32,1,128]{3,2,1,0:T(1,128)S(1)}, u32[]{:S(2)}, u32[]{:S(2)}) collective-permute-start(f32[3,32,1,128]{3,2,1,0:T(1,128)S(1)} %slice.668), channel_id=1, source_target_pairs={{1,0},{2,1},{3,2},{5,4},{6,5},{7,6},{9,8},{10,9},{11,10},{13,12},{... | collective-permute-start | bytes 147464 | tf_op jit(solution)/shard_map/ppermute | solution.py:25
  38.3 5.6 %collective-permute-start.8 = (f32[3,1,8,128]{3,2,1,0:T(8,128)S(1)}, f32[3,1,8,128]{3,2,1,0:T(8,128)S(1)}, u32[]{:S(2)}, u32[]{:S(2)}) collective-permute-start(f32[3,1,8,128]{3,2,1,0:T(8,128)S(1)} %slice.674), channel_id=1, source_target_pairs={{4,0},{5,1},{6,2},{7,3},{12,8},{13,9},{14,10},{15,11},{20,16},{21,... | collective-permute-start | bytes 36872 | tf_op jit(solution)/shard_map/ppermute | solution.py:25
  44.1 7.3 %copy-start.2 = (f32[1,3,32,8,128]{4,3,2,1,0:T(8,128)S(1)}, f32[1,3,32,8,128]{4,3,2,1,0:T(8,128)}, u32[]{:S(2)}) copy-start(f32[1,3,32,8,128]{4,3,2,1,0:T(8,128)} %param.18) | copy-start | bytes 1179652
  44.2 12.6 %collective-permute-start.9 = (f32[3,32,1,128]{3,2,1,0:T(1,128)S(1)}, f32[3,32,1,128]{3,2,1,0:T(1,128)S(1)}, u32[]{:S(2)}, u32[]{:S(2)}) collective-permute-start(f32[3,32,1,128]{3,2,1,0:T(1,128)S(1)} %slice.678), channel_id=1, source_target_pairs={{0,1},{1,2},{2,3},{4,5},{5,6},{6,7},{8,9},{9,10},{10,11},{12,13},{... | collective-permute-start | bytes 147464 | tf_op jit(solution)/shard_map/ppermute | solution.py:25
  48.8 8.0 %collective-permute-start.10 = (f32[3,1,8,128]{3,2,1,0:T(8,128)S(1)}, f32[3,1,8,128]{3,2,1,0:T(8,128)S(1)}, u32[]{:S(2)}, u32[]{:S(2)}) collective-permute-start(f32[3,1,8,128]{3,2,1,0:T(8,128)S(1)} %slice.684), channel_id=1, source_target_pairs={{0,4},{1,5},{2,6},{3,7},{8,12},{9,13},{10,14},{11,15},{16,20},{17,... | collective-permute-start | bytes 36872 | tf_op jit(solution)/shard_map/ppermute | solution.py:25
  51.5 8.4 %collective-permute-start.17 = (f32[3,32,1,128]{3,2,1,0:T(1,128)S(1)}, f32[3,32,1,128]{3,2,1,0:T(1,128)S(1)}, u32[]{:S(2)}, u32[]{:S(2)}) collective-permute-start(f32[3,32,1,128]{3,2,1,0:T(1,128)S(1)} %slice.724), channel_id=1, source_target_pairs={{0,1},{1,2},{2,3},{4,5},{5,6},{6,7},{8,9},{9,10},{10,11},{12,13},{... | collective-permute-start | bytes 147464 | tf_op jit(solution)/shard_map/ppermute | solution.py:25
  55.4 4.5 %collective-permute-start.18 = (f32[3,1,8,128]{3,2,1,0:T(8,128)S(1)}, f32[3,1,8,128]{3,2,1,0:T(8,128)S(1)}, u32[]{:S(2)}, u32[]{:S(2)}) collective-permute-start(f32[3,1,8,128]{3,2,1,0:T(8,128)S(1)} %slice.730), channel_id=1, source_target_pairs={{0,4},{1,5},{2,6},{3,7},{8,12},{9,13},{10,14},{11,15},{16,20},{17,... | collective-permute-start | bytes 36872 | tf_op jit(solution)/shard_map/ppermute | solution.py:25
  57.3 6.9 %collective-permute-start.11 = (f32[3,32,1,128]{3,2,1,0:T(1,128)S(1)}, f32[3,32,1,128]{3,2,1,0:T(1,128)S(1)}, u32[]{:S(2)}, u32[]{:S(2)}) collective-permute-start(f32[3,32,1,128]{3,2,1,0:T(1,128)S(1)} %slice.691), channel_id=1, source_target_pairs={{1,0},{2,1},{3,2},{5,4},{6,5},{7,6},{9,8},{10,9},{11,10},{13,12},{... | collective-permute-start | bytes 147464 | tf_op jit(solution)/shard_map/ppermute | solution.py:25
  58.6 5.6 %collective-permute-start.12 = (f32[3,1,8,128]{3,2,1,0:T(8,128)S(1)}, f32[3,1,8,128]{3,2,1,0:T(8,128)S(1)}, u32[]{:S(2)}, u32[]{:S(2)}) collective-permute-start(f32[3,1,8,128]{3,2,1,0:T(8,128)S(1)} %slice.697), channel_id=1, source_target_pairs={{4,0},{5,1},{6,2},{7,3},{12,8},{13,9},{14,10},{15,11},{20,16},{21,... | collective-permute-start | bytes 36872 | tf_op jit(solution)/shard_map/ppermute | solution.py:25
  64.5 7.6 %collective-permute-start.13 = (f32[3,32,1,128]{3,2,1,0:T(1,128)S(1)}, f32[3,32,1,128]{3,2,1,0:T(1,128)S(1)}, u32[]{:S(2)}, u32[]{:S(2)}) collective-permute-start(f32[3,32,1,128]{3,2,1,0:T(1,128)S(1)} %slice.701), channel_id=1, source_target_pairs={{0,1},{1,2},{2,3},{4,5},{5,6},{6,7},{8,9},{9,10},{10,11},{12,13},{... | collective-permute-start | bytes 147464 | tf_op jit(solution)/shard_map/ppermute | solution.py:25
  69.1 3.0 %collective-permute-start.14 = (f32[3,1,8,128]{3,2,1,0:T(8,128)S(1)}, f32[3,1,8,128]{3,2,1,0:T(8,128)S(1)}, u32[]{:S(2)}, u32[]{:S(2)}) collective-permute-start(f32[3,1,8,128]{3,2,1,0:T(8,128)S(1)} %slice.707), channel_id=1, source_target_pairs={{0,4},{1,5},{2,6},{3,7},{8,12},{9,13},{10,14},{11,15},{16,20},{17,... | collective-permute-start | bytes 36872 | tf_op jit(solution)/shard_map/ppermute | solution.py:25
  72.6 0.8 copy-start.4
  73.4 15.5 %copy-start.17 = (f32[3,32,8]{2,1,0:T(8,128)}, f32[3,32,8]{2,1,0:T(8,128)S(1)}, u32[]{:S(2)}) copy-start(f32[3,32,8]{2,1,0:T(8,128)S(1)} %get-tuple-element.46) | copy-start | bytes 9220
  73.4 15.5 %copy-start.20 = (f32[3,32,8]{2,1,0:T(8,128)}, f32[3,32,8]{2,1,0:T(8,128)S(1)}, u32[]{:S(2)}) copy-start(f32[3,32,8]{2,1,0:T(8,128)S(1)} %get-tuple-element.45) | copy-start | bytes 9220
  73.7 6.9 %collective-permute-start.19 = (f32[3,32,1,128]{3,2,1,0:T(1,128)S(1)}, f32[3,32,1,128]{3,2,1,0:T(1,128)S(1)}, u32[]{:S(2)}, u32[]{:S(2)}) collective-permute-start(f32[3,32,1,128]{3,2,1,0:T(1,128)S(1)} %slice.736), channel_id=1, source_target_pairs={{1,0},{2,1},{3,2},{5,4},{6,5},{7,6},{9,8},{10,9},{11,10},{13,12},{... | collective-permute-start | bytes 147464 | tf_op jit(solution)/shard_map/ppermute | solution.py:25
  75.0 5.6 %collective-permute-start.20 = (f32[3,1,8,128]{3,2,1,0:T(8,128)S(1)}, f32[3,1,8,128]{3,2,1,0:T(8,128)S(1)}, u32[]{:S(2)}, u32[]{:S(2)}) collective-permute-start(f32[3,1,8,128]{3,2,1,0:T(8,128)S(1)} %slice.742), channel_id=1, source_target_pairs={{4,0},{5,1},{6,2},{7,3},{12,8},{13,9},{14,10},{15,11},{20,16},{21,... | collective-permute-start | bytes 36872 | tf_op jit(solution)/shard_map/ppermute | solution.py:25
  80.9 7.7 %copy-start.6 = (f32[1,32,8,128]{3,2,1,0:T(8,128)}, f32[1,32,8,128]{3,2,1,0:T(8,128)S(1)}, u32[]{:S(2)}) copy-start(f32[1,32,8,128]{3,2,1,0:T(8,128)S(1)} %get-tuple-element.67) | copy-start | bytes 393220
  81.0 7.6 %collective-permute-start.21 = (f32[3,32,1,128]{3,2,1,0:T(1,128)S(1)}, f32[3,32,1,128]{3,2,1,0:T(1,128)S(1)}, u32[]{:S(2)}, u32[]{:S(2)}) collective-permute-start(f32[3,32,1,128]{3,2,1,0:T(1,128)S(1)} %slice.746), channel_id=1, source_target_pairs={{0,1},{1,2},{2,3},{4,5},{5,6},{6,7},{8,9},{9,10},{10,11},{12,13},{... | collective-permute-start | bytes 147464 | tf_op jit(solution)/shard_map/ppermute | solution.py:25
  85.6 3.0 %collective-permute-start.22 = (f32[3,1,8,128]{3,2,1,0:T(8,128)S(1)}, f32[3,1,8,128]{3,2,1,0:T(8,128)S(1)}, u32[]{:S(2)}, u32[]{:S(2)}) collective-permute-start(f32[3,1,8,128]{3,2,1,0:T(8,128)S(1)} %slice.752), channel_id=1, source_target_pairs={{0,4},{1,5},{2,6},{3,7},{8,12},{9,13},{10,14},{11,15},{16,20},{17,... | collective-permute-start | bytes 36872 | tf_op jit(solution)/shard_map/ppermute | solution.py:25
  88.9 0.7 copy-start.8
  88.9 0.7 copy-start.11
  88.9 0.7 copy-start.14
  90.3 7.0 %collective-permute-start.23 = (f32[3,32,1,128]{3,2,1,0:T(1,128)}, f32[3,32,1,128]{3,2,1,0:T(1,128)}, u32[]{:S(2)}, u32[]{:S(2)}) collective-permute-start(f32[3,32,1,128]{3,2,1,0:T(1,128)} %slice.758), channel_id=1, source_target_pairs={{1,0},{2,1},{3,2},{5,4},{6,5},{7,6},{9,8},{10,9},{11,10},{13,12},{... | collective-permute-start | bytes 147464 | tf_op jit(solution)/shard_map/ppermute | solution.py:25
  91.6 5.7 %collective-permute-start.24 = (f32[3,1,8,128]{3,2,1,0:T(8,128)S(1)}, f32[3,1,8,128]{3,2,1,0:T(8,128)}, u32[]{:S(2)}, u32[]{:S(2)}) collective-permute-start(f32[3,1,8,128]{3,2,1,0:T(8,128)S(1)} %slice.764), channel_id=1, source_target_pairs={{4,0},{5,1},{6,2},{7,3},{12,8},{13,9},{14,10},{15,11},{20,16},{21,... | collective-permute-start | bytes 36872 | tf_op jit(solution)/shard_map/ppermute | solution.py:25
  93.8 3.5 %copy-start.9 = (f32[1,32,8,128]{3,2,1,0:T(8,128)S(1)}, f32[1,32,8,128]{3,2,1,0:T(8,128)}, u32[]{:S(2)}) copy-start(f32[1,32,8,128]{3,2,1,0:T(8,128)} %copy-done.8) | copy-start | bytes 393220
  93.8 3.5 %copy-start.12 = (f32[1,32,8,128]{3,2,1,0:T(8,128)S(1)}, f32[1,32,8,128]{3,2,1,0:T(8,128)}, u32[]{:S(2)}) copy-start(f32[1,32,8,128]{3,2,1,0:T(8,128)} %copy-done.11) | copy-start | bytes 393220
  93.8 3.5 %copy-start.15 = (f32[1,32,8,128]{3,2,1,0:T(8,128)S(1)}, f32[1,32,8,128]{3,2,1,0:T(8,128)}, u32[]{:S(2)}) copy-start(f32[1,32,8,128]{3,2,1,0:T(8,128)} %copy-done.14) | copy-start | bytes 393220
  93.8 3.5 %copy-start.18 = (f32[3,32,8]{2,1,0:T(8,128)S(1)}, f32[3,32,8]{2,1,0:T(8,128)}, u32[]{:S(2)}) copy-start(f32[3,32,8]{2,1,0:T(8,128)} %copy-done.17) | copy-start | bytes 9220
  93.8 3.5 %copy-start.21 = (f32[3,32,8]{2,1,0:T(8,128)S(1)}, f32[3,32,8]{2,1,0:T(8,128)}, u32[]{:S(2)}) copy-start(f32[3,32,8]{2,1,0:T(8,128)} %copy-done.20) | copy-start | bytes 9220
  98.5 0.9 copy-start.7
  99.4 7.4 %copy-start.5 = (f32[3,32,8,128]{3,2,1,0:T(8,128)S(1)}, f32[3,32,8,128]{3,2,1,0:T(8,128)}, u32[]{:S(2)}) copy-start(f32[3,32,8,128]{3,2,1,0:T(8,128)} %copy-done.4) | copy-start | bytes 1179652
  99.5 8.6 %collective-permute-start.25 = (f32[3,32,1,128]{3,2,1,0:T(1,128)S(1)}, f32[3,32,1,128]{3,2,1,0:T(1,128)S(1)}, u32[]{:S(2)}, u32[]{:S(2)}) collective-permute-start(f32[3,32,1,128]{3,2,1,0:T(1,128)S(1)} %slice.768), channel_id=1, source_target_pairs={{0,1},{1,2},{2,3},{4,5},{5,6},{6,7},{8,9},{9,10},{10,11},{12,13},{... | collective-permute-start | bytes 147464 | tf_op jit(solution)/shard_map/ppermute | solution.py:25
  104.1 4.0 %collective-permute-start.26 = (f32[3,1,8,128]{3,2,1,0:T(8,128)S(1)}, f32[3,1,8,128]{3,2,1,0:T(8,128)S(1)}, u32[]{:S(2)}, u32[]{:S(2)}) collective-permute-start(f32[3,1,8,128]{3,2,1,0:T(8,128)S(1)} %slice.774), channel_id=1, source_target_pairs={{0,4},{1,5},{2,6},{3,7},{8,12},{9,13},{10,14},{11,15},{16,20},{17,... | collective-permute-start | bytes 36872 | tf_op jit(solution)/shard_map/ppermute | solution.py:25
  108.4 0.8 copy-start.24
  108.5 0.7 copy-start.27
  109.8 12.6 %copy-start.19 = (f32[3,32,8]{2,1,0:T(8,128)S(1)}, f32[3,32,8]{2,1,0:T(8,128)}, u32[]{:S(2)}) copy-start(f32[3,32,8]{2,1,0:T(8,128)} %copy-done.17) | copy-start | bytes 9220
  109.8 12.6 %copy-start.22 = (f32[3,32,8]{2,1,0:T(8,128)S(1)}, f32[3,32,8]{2,1,0:T(8,128)}, u32[]{:S(2)}) copy-start(f32[3,32,8]{2,1,0:T(8,128)} %copy-done.20) | copy-start | bytes 9220
  121.6 0.9 copy-start.13
  121.6 1.0 copy-start.16
  121.7 0.9 copy-start.10
